TPU v7x, 256 devices: a whole 4x4x8 slice. The times are simulated.
256 devices in a mesh: seq: 32 (over z, x_lo, core), dp: 8 (over y, x_hi).
Axes of the slice: x: 4 (x_hi: 2, x_lo: 2; x = x_hi * 2 + x_lo), y: 4, z: 8, core: 2. Of those that a mesh axis runs over, the one named last changes fastest.
Arguments:
- queries: bfloat16 [8, 4096, 2048], P('dp', 'seq'), may hold values from -18 to 18
- key_vectors: bfloat16 [8, 4096, 2048], P('dp', 'seq'), may hold values from -18 to 18
- value_vectors: bfloat16 [8, 4096, 2048], P('dp', 'seq'), may hold values from -6 to 6
- cotangent: bfloat16 [8, 4096, 2048], P('dp', 'seq'), may hold values from -6 to 6
- compress_kernel: bfloat16 [512, 128], replicated, may hold values from -0.25 to 0.25
- memory_reach: int32 [8, 32], P('dp', 'seq'), may hold values from 1 to 4, as said below
Outputs:
- attended: bfloat16 [8, 4096, 2048], P('dp', 'seq')
- grad_queries: bfloat16 [8, 4096, 2048], P('dp', 'seq')
- grad_keys: bfloat16 [8, 4096, 2048], P('dp', 'seq')
- grad_values: bfloat16 [8, 4096, 2048], P('dp', 'seq')
- grad_kernel: float32 [512, 128], P('seq')
Inputs may be any that keep to these rules, and one draw needn't show every extreme that they name: `memory_reach`: some segment reads 4 earlier segments and some reads 1.
All inputs are finite; a program needn't handle non-finite values.
Results may differ from a plain program's by a relative error of at most 0.0076.
Values may be sent and summed in bfloat16 or wider, within the bound.
A program may use at most 64 MiB of HBM per device.

v0:
```python
import jax
import jax.numpy as jnp
from jax import lax
from jax.sharding import PartitionSpec as P

H = 16
E = 128


def shifted(value, axis, steps):
    count = lax.axis_size(axis)
    initial, last = (max(0, -steps), min(count, count - steps))
    return lax.ppermute(value, axis, [(source, source + steps) for source in range(initial, last)])


def attend_block(query_rows, key_rows, value_rows, grad_rows, memory_keys, memory_values, visible):
    segment_len = query_rows.shape[0]
    slot_rows = segment_len // 4
    span_len = 2 * segment_len
    score_scale = E ** (-0.5)
    query_heads = query_rows.reshape(segment_len, H, E)
    grad_heads = grad_rows.reshape(segment_len, H, E)
    key_heads = jnp.concatenate([memory_keys, key_rows], 0).reshape(span_len, H, E)
    value_heads = jnp.concatenate([memory_values, value_rows], 0).reshape(span_len, H, E)
    columns = jnp.arange(span_len, dtype=jnp.int32)
    row_ids = jnp.arange(segment_len, dtype=jnp.int32)
    slot_of = jnp.minimum(columns // slot_rows, 3)
    memory_open = jnp.any(
        (slot_of[:, None] == jnp.arange(4, dtype=jnp.int32)[None, :]) & visible[None, :], axis=1
    )
    allowed = jnp.where(
        columns[None, :] < segment_len,
        memory_open[None, :],
        columns[None, :] - segment_len <= row_ids[:, None],
    )
    scores = (
        jnp.einsum("shd,lhd->hsl", query_heads, key_heads, preferred_element_type=jnp.float32)
        * score_scale
    )
    scores = jnp.where(allowed[None], scores, -1e30)
    highest = jnp.max(scores, axis=2, keepdims=True)
    raised = jnp.where(allowed[None], jnp.exp(scores - highest), 0.0)
    weights = raised / jnp.sum(raised, axis=2, keepdims=True)
    weights_low = weights.astype(jnp.bfloat16)
    attended = jnp.einsum(
        "hsl,lhd->shd", weights_low, value_heads, preferred_element_type=jnp.float32
    )
    grad_weights = jnp.einsum(
        "shd,lhd->hsl", grad_heads, value_heads, preferred_element_type=jnp.float32
    )
    row_delta = jnp.sum(weights * grad_weights, axis=2, keepdims=True)
    grad_scores = (weights * (grad_weights - row_delta) * score_scale).astype(jnp.bfloat16)
    grad_query = jnp.einsum(
        "hsl,lhd->shd", grad_scores, key_heads, preferred_element_type=jnp.float32
    )
    grad_key_list = jnp.einsum(
        "hsl,shd->lhd", grad_scores, query_heads, preferred_element_type=jnp.float32
    ).reshape(span_len, H * E)
    grad_value_list = jnp.einsum(
        "hsl,shd->lhd", weights_low, grad_heads, preferred_element_type=jnp.float32
    ).reshape(span_len, H * E)
    return (
        attended.reshape(segment_len, H * E).astype(jnp.bfloat16),
        grad_query.reshape(segment_len, H * E).astype(jnp.bfloat16),
        grad_key_list[segment_len:],
        grad_value_list[segment_len:],
        grad_key_list[:segment_len],
        grad_value_list[:segment_len],
    )


def local(queries, key_vectors, value_vectors, cotangent, compress_kernel, memory_reach):
    query_rows = queries[0]
    key_rows = key_vectors[0]
    value_rows = value_vectors[0]
    grad_rows = cotangent[0]
    segment_len = query_rows.shape[0]
    slot_rows = segment_len // 4
    kernel = compress_kernel.reshape(4, E, E)
    key_blocks = key_rows.reshape(slot_rows, 4, H, E)
    value_blocks = value_rows.reshape(slot_rows, 4, H, E)
    packed_keys = (
        jnp.einsum("mthe,tef->mhf", key_blocks, kernel, preferred_element_type=jnp.float32)
        .astype(jnp.bfloat16)
        .reshape(slot_rows, H * E)
    )
    packed_values = (
        jnp.einsum("mthe,tef->mhf", value_blocks, kernel, preferred_element_type=jnp.float32)
        .astype(jnp.bfloat16)
        .reshape(slot_rows, H * E)
    )
    received = []
    for offset in range(1, 5):
        received.append(shifted((packed_keys, packed_values), "seq", offset))
    memory_keys = jnp.concatenate([shifted_pair[0] for shifted_pair in received], 0)
    memory_values = jnp.concatenate([shifted_pair[1] for shifted_pair in received], 0)
    position = lax.axis_index("seq")
    slot_ids = jnp.arange(1, 5, dtype=jnp.int32)
    visible = (slot_ids <= memory_reach[0, 0]) & (position - slot_ids >= 0)
    attended, grad_query, local_keys, local_values, memory_grad_keys, memory_grad_values = (
        attend_block(
            query_rows, key_rows, value_rows, grad_rows, memory_keys, memory_values, visible
        )
    )
    slot_keys = memory_grad_keys.reshape(4, slot_rows, H * E)
    slot_values = memory_grad_values.reshape(4, slot_rows, H * E)
    summed_keys = jnp.zeros((slot_rows, H * E), jnp.float32)
    summed_values = jnp.zeros((slot_rows, H * E), jnp.float32)
    for offset in range(1, 5):
        arrived = shifted((slot_keys[offset - 1], slot_values[offset - 1]), "seq", -offset)
        summed_keys = summed_keys + arrived[0]
        summed_values = summed_values + arrived[1]
    packed_grad_keys = summed_keys.astype(jnp.bfloat16).reshape(slot_rows, H, E)
    packed_grad_values = summed_values.astype(jnp.bfloat16).reshape(slot_rows, H, E)
    back_keys = jnp.einsum(
        "mhf,tef->mthe", packed_grad_keys, kernel, preferred_element_type=jnp.float32
    ).reshape(segment_len, H * E)
    back_values = jnp.einsum(
        "mhf,tef->mthe", packed_grad_values, kernel, preferred_element_type=jnp.float32
    ).reshape(segment_len, H * E)
    key_grad = (local_keys + back_keys).astype(jnp.bfloat16)
    value_grad = (local_values + back_values).astype(jnp.bfloat16)
    kernel_terms = (
        jnp.einsum(
            "mthe,mhf->tef", key_blocks, packed_grad_keys, preferred_element_type=jnp.float32
        )
        + jnp.einsum(
            "mthe,mhf->tef", value_blocks, packed_grad_values, preferred_element_type=jnp.float32
        )
    ).reshape(4 * E, E)
    whole_sum = lax.psum(kernel_terms, ("seq", "dp"))
    share_rows = 4 * E // lax.axis_size("seq")
    grad_kernel = lax.dynamic_slice_in_dim(
        whole_sum, lax.axis_index("seq") * share_rows, share_rows, 0
    )
    return (attended[None], grad_query[None], key_grad[None], value_grad[None], grad_kernel)


def solution(mesh):
    return jax.shard_map(
        local,
        mesh=mesh,
        in_specs=(
            P("dp", "seq", None),
            P("dp", "seq", None),
            P("dp", "seq", None),
            P("dp", "seq", None),
            P(),
            P("dp", "seq"),
        ),
        out_specs=(
            P("dp", "seq", None),
            P("dp", "seq", None),
            P("dp", "seq", None),
            P("dp", "seq", None),
            P("seq", None),
        ),
        check_vma=False,
    )
```

profile of v0, /device:TPU:1, one launch (start us, length us, event | category | flops | bytes accessed | tf_op | source)
XLA Modules:
  0.0 405.9 jit_solution(10729442592492152735)
XLA Ops:
  9.5 4.4 %collective-permute-start.3 = (bf16[32,2048]{1,0:T(8,128)(2,1)}, bf16[32,2048]{1,0:T(8,128)(2,1)S(1)}, u32[]{:S(2)}, u32[]{:S(2)}) collective-permute-start(bf16[32,2048]{1,0:T(8,128)(2,1)} %bitcast.202), channel_id=1, source_target_pairs={{0,32},{8,40},{16,48},{24,56},{32,64},{40,72},{48,80},{56,88},{64,... | collective-permute-start | bytes 393224 | tf_op jit(solution)/shard_map/ppermute | solution.py:13
  13.8 4.4 %collective-permute-start.2 = (bf16[32,2048]{1,0:T(8,128)(2,1)}, bf16[32,2048]{1,0:T(8,128)(2,1)S(1)}, u32[]{:S(2)}, u32[]{:S(2)}) collective-permute-start(bf16[32,2048]{1,0:T(8,128)(2,1)} %bitcast.202), channel_id=1, source_target_pairs={{0,24},{8,32},{16,40},{24,48},{32,56},{40,64},{48,72},{56,80},{64,... | collective-permute-start | bytes 393224 | tf_op jit(solution)/shard_map/ppermute | solution.py:13
  18.2 3.8 collective-permute-start.1
  22.0 2.2 collective-permute-start
  25.3 3.0 collective-permute-start.4
  33.3 3.1 collective-permute-start.5
  37.3 2.4 collective-permute-done.5
  39.7 5.3 %collective-permute-start.6 = (bf16[32,2048]{1,0:T(8,128)(2,1)}, bf16[32,2048]{1,0:T(8,128)(2,1)S(1)}, u32[]{:S(2)}, u32[]{:S(2)}) collective-permute-start(bf16[32,2048]{1,0:T(8,128)(2,1)} %bitcast.201), channel_id=1, source_target_pairs={{0,24},{8,32},{16,40},{24,48},{32,56},{40,64},{48,72},{56,80},{64,... | collective-permute-start | bytes 393224 | tf_op jit(solution)/shard_map/ppermute | solution.py:13
  45.1 2.2 collective-permute-done.6
  47.3 6.0 %collective-permute-start.7 = (bf16[32,2048]{1,0:T(8,128)(2,1)}, bf16[32,2048]{1,0:T(8,128)(2,1)S(1)}, u32[]{:S(2)}, u32[]{:S(2)}) collective-permute-start(bf16[32,2048]{1,0:T(8,128)(2,1)} %bitcast.201), channel_id=1, source_target_pairs={{0,32},{8,40},{16,48},{24,56},{32,64},{40,72},{48,80},{56,88},{64,... | collective-permute-start | bytes 393224 | tf_op jit(solution)/shard_map/ppermute | solution.py:13
  53.3 2.5 collective-permute-done.7
  62.2 2.8 concatenate.33
  65.0 2.9 fusion.18
  67.9 3.5 fusion.45
  71.4 3.0 convolution_convert_fusion.1
  74.9 6.5 %convolution_bitcast_fusion.1 = f32[256,16,128]{2,0,1:T(8,128)} fusion(f32[16,256,128]{2,1,0:T(8,128)} %fusion.18, bf16[128,16,128]{2,1,0:T(8,128)(2,1)} %bitcast.229, f32[16,128,256]{1,2,0:T(8,128)} %get-tuple-element.29, f32[16,128]{1,0:T(8,128)S(1)} %get-tuple-element.28), kind=kOutput, calls=%fused_computation.11 | convolution fusion | flops 137890048 | bytes 6823936 | tf_op jit(solution)/shard_map/hsl,shd->lhd/dot_general | solution.py:56
  90.1 5.6 %convolution_convert_fusion = bf16[16,128,128]{2,1,0:T(8,128)(2,1)} fusion(bf16[256,16,128]{2,0,1:T(8,128)(2,1)} %constant_dynamic-update-slice_fusion, f32[16,256,128]{2,1,0:T(8,128)} %fusion.18, f32[16,128,256]{1,2,0:T(8,128)} %get-tuple-element.29, f32[16,128]{1,0:T(8,128)S(1)} %get-tuple-element.28), kind=kOutput, calls=%fused_computation.14 | convolution fusion | flops 138152192 | bytes 5775360 | tf_op jit(solution)/shard_map/hsl,lhd->shd/dot_general | solution.py:53
  95.7 2.1 copy.102
  97.8 2.0 copy.103
  117.6 2.5 copy.99
  120.4 5.8 %collective-permute-done.10 = f32[32,2048]{1,0:T(8,128)} collective-permute-done((f32[32,2048]{1,0:T(8,128)}, f32[32,2048]{1,0:T(8,128)}, u32[]{:S(2)}, u32[]{:S(2)}) %collective-permute-start.10) | collective-permute-done | bytes 262176 | tf_op jit(solution)/shard_map/ppermute | solution.py:13
  126.3 4.1 %collective-permute-done.11 = f32[32,2048]{1,0:T(8,128)} collective-permute-done((f32[32,2048]{1,0:T(8,128)}, f32[32,2048]{1,0:T(8,128)}, u32[]{:S(2)}, u32[]{:S(2)}) %collective-permute-start.11) | collective-permute-done | bytes 262176 | tf_op jit(solution)/shard_map/ppermute | solution.py:13
  134.2 2.7 copy.92
  141.3 256.5 %all-reduce.2.cloned.1.call-done = f32[512,128]{1,0:T(8,128)} async-done(((f32[512,128]{1,0:T(8,128)}), f32[512,128]{1,0:T(8,128)}) %all-reduce.2.cloned.1.call-update) | async-done | bytes 262160 | tf_op jit(solution)/shard_map/psum | solution.py:131
  (111 shorter events, 51.7 us)
Async XLA Ops:
  7.2 17.0 %copy-start.8 = (bf16[1,128,2048]{2,1,0:T(8,128)(2,1)S(1)}, bf16[1,128,2048]{2,1,0:T(8,128)(2,1)}, u32[]{:S(2)}) copy-start(bf16[1,128,2048]{2,1,0:T(8,128)(2,1)} %param.7) | copy-start | bytes 1572868
  7.2 390.6 %all-reduce.2.cloned.1.call-start = ((), (), s32[]{:S(2)}) async-start(), calls=%async_computation | async-start | bytes 524288 | tf_op jit(solution)/shard_map/psum | solution.py:131
  8.5 20.2 %copy-start.9 = (bf16[1,128,2048]{2,1,0:T(8,128)(2,1)S(1)}, bf16[1,128,2048]{2,1,0:T(8,128)(2,1)}, u32[]{:S(2)}) copy-start(bf16[1,128,2048]{2,1,0:T(8,128)(2,1)} %param.8) | copy-start | bytes 1572868
  9.5 51.7 %collective-permute-start.3 = (bf16[32,2048]{1,0:T(8,128)(2,1)}, bf16[32,2048]{1,0:T(8,128)(2,1)S(1)}, u32[]{:S(2)}, u32[]{:S(2)}) collective-permute-start(bf16[32,2048]{1,0:T(8,128)(2,1)} %bitcast.202), channel_id=1, source_target_pairs={{0,32},{8,40},{16,48},{24,56},{32,64},{40,72},{48,80},{56,88},{64,... | collective-permute-start | bytes 393224 | tf_op jit(solution)/shard_map/ppermute | solution.py:13
  13.8 45.4 %collective-permute-start.2 = (bf16[32,2048]{1,0:T(8,128)(2,1)}, bf16[32,2048]{1,0:T(8,128)(2,1)S(1)}, u32[]{:S(2)}, u32[]{:S(2)}) collective-permute-start(bf16[32,2048]{1,0:T(8,128)(2,1)} %bitcast.202), channel_id=1, source_target_pairs={{0,24},{8,32},{16,40},{24,48},{32,56},{40,64},{48,72},{56,80},{64,... | collective-permute-start | bytes 393224 | tf_op jit(solution)/shard_map/ppermute | solution.py:13
  18.2 39.8 %collective-permute-start.1 = (bf16[32,2048]{1,0:T(8,128)(2,1)}, bf16[32,2048]{1,0:T(8,128)(2,1)}, u32[]{:S(2)}, u32[]{:S(2)}) collective-permute-start(bf16[32,2048]{1,0:T(8,128)(2,1)} %bitcast.202), channel_id=1, source_target_pairs={{0,16},{8,24},{16,32},{24,40},{32,48},{40,56},{48,64},{56,72},{64,... | collective-permute-start | bytes 393224 | tf_op jit(solution)/shard_map/ppermute | solution.py:13
  22.0 34.9 %collective-permute-start = (bf16[32,2048]{1,0:T(8,128)(2,1)}, bf16[32,2048]{1,0:T(8,128)(2,1)}, u32[]{:S(2)}, u32[]{:S(2)}) collective-permute-start(bf16[32,2048]{1,0:T(8,128)(2,1)} %bitcast.202), channel_id=1, source_target_pairs={{0,8},{8,16},{16,24},{24,32},{32,40},{40,48},{48,56},{56,64},{64,7... | collective-permute-start | bytes 393224 | tf_op jit(solution)/shard_map/ppermute | solution.py:13
  24.2 6.1 %copy-start.10 = (bf16[1,128,2048]{2,1,0:T(8,128)(2,1)S(1)}, bf16[1,128,2048]{2,1,0:T(8,128)(2,1)}, u32[]{:S(2)}) copy-start(bf16[1,128,2048]{2,1,0:T(8,128)(2,1)} %param.6) | copy-start | bytes 1572868
  25.3 8.0 %collective-permute-start.4 = (bf16[32,2048]{1,0:T(8,128)(2,1)}, bf16[32,2048]{1,0:T(8,128)(2,1)}, u32[]{:S(2)}, u32[]{:S(2)}) collective-permute-start(bf16[32,2048]{1,0:T(8,128)(2,1)} %bitcast.201), channel_id=1, source_target_pairs={{0,8},{8,16},{16,24},{24,32},{32,40},{40,48},{48,56},{56,64},{64,7... | collective-permute-start | bytes 393224 | tf_op jit(solution)/shard_map/ppermute | solution.py:13
  33.3 6.5 %collective-permute-start.5 = (bf16[32,2048]{1,0:T(8,128)(2,1)}, bf16[32,2048]{1,0:T(8,128)(2,1)S(1)}, u32[]{:S(2)}, u32[]{:S(2)}) collective-permute-start(bf16[32,2048]{1,0:T(8,128)(2,1)} %bitcast.201), channel_id=1, source_target_pairs={{0,16},{8,24},{16,32},{24,40},{32,48},{40,56},{48,64},{56,72},{64,... | collective-permute-start | bytes 393224 | tf_op jit(solution)/shard_map/ppermute | solution.py:13
  39.7 7.5 %collective-permute-start.6 = (bf16[32,2048]{1,0:T(8,128)(2,1)}, bf16[32,2048]{1,0:T(8,128)(2,1)S(1)}, u32[]{:S(2)}, u32[]{:S(2)}) collective-permute-start(bf16[32,2048]{1,0:T(8,128)(2,1)} %bitcast.201), channel_id=1, source_target_pairs={{0,24},{8,32},{16,40},{24,48},{32,56},{40,64},{48,72},{56,80},{64,... | collective-permute-start | bytes 393224 | tf_op jit(solution)/shard_map/ppermute | solution.py:13
  47.3 8.5 %collective-permute-start.7 = (bf16[32,2048]{1,0:T(8,128)(2,1)}, bf16[32,2048]{1,0:T(8,128)(2,1)S(1)}, u32[]{:S(2)}, u32[]{:S(2)}) collective-permute-start(bf16[32,2048]{1,0:T(8,128)(2,1)} %bitcast.201), channel_id=1, source_target_pairs={{0,32},{8,40},{16,48},{24,56},{32,64},{40,72},{48,80},{56,88},{64,... | collective-permute-start | bytes 393224 | tf_op jit(solution)/shard_map/ppermute | solution.py:13
  74.9 20.8 %copy-start.4 = (f32[256,16,128]{2,0,1:T(8,128)}, f32[256,16,128]{2,0,1:T(8,128)S(1)}, u32[]{:S(2)}) copy-start(f32[256,16,128]{2,0,1:T(8,128)S(1)} %convolution_bitcast_fusion) | copy-start | bytes 6291460
  84.3 26.4 %collective-permute-start.12 = (f32[32,2048]{1,0:T(8,128)}, f32[32,2048]{1,0:T(8,128)}, u32[]{:S(2)}, u32[]{:S(2)}) collective-permute-start(f32[32,2048]{1,0:T(8,128)} %bitcast.196), channel_id=1, source_target_pairs={{8,0},{16,8},{24,16},{32,24},{40,32},{48,40},{56,48},{64,56},{72,6... | collective-permute-start | bytes 786440 | tf_op jit(solution)/shard_map/ppermute | solution.py:13
  86.2 25.8 %collective-permute-start.14 = (f32[32,2048]{1,0:T(8,128)}, f32[32,2048]{1,0:T(8,128)}, u32[]{:S(2)}, u32[]{:S(2)}) collective-permute-start(f32[32,2048]{1,0:T(8,128)} %bitcast.194), channel_id=1, source_target_pairs={{24,0},{32,8},{40,16},{48,24},{56,32},{64,40},{72,48},{80,56},{88,... | collective-permute-start | bytes 786440 | tf_op jit(solution)/shard_map/ppermute | solution.py:13
  87.5 25.8 %collective-permute-start.15 = (f32[32,2048]{1,0:T(8,128)}, f32[32,2048]{1,0:T(8,128)}, u32[]{:S(2)}, u32[]{:S(2)}) collective-permute-start(f32[32,2048]{1,0:T(8,128)} %bitcast.193), channel_id=1, source_target_pairs={{32,0},{40,8},{48,16},{56,24},{64,32},{72,40},{80,48},{88,56},{96,... | collective-permute-start | bytes 786440 | tf_op jit(solution)/shard_map/ppermute | solution.py:13
  88.8 26.0 %collective-permute-start.13 = (f32[32,2048]{1,0:T(8,128)}, f32[32,2048]{1,0:T(8,128)}, u32[]{:S(2)}, u32[]{:S(2)}) collective-permute-start(f32[32,2048]{1,0:T(8,128)} %bitcast.195), channel_id=1, source_target_pairs={{16,0},{24,8},{32,16},{40,24},{48,32},{56,40},{64,48},{72,56},{80,... | collective-permute-start | bytes 786440 | tf_op jit(solution)/shard_map/ppermute | solution.py:13
  95.7 4.2 %slice-start.1 = ((f32[256,16,128]{2,0,1:T(8,128)}), f32[128,16,128]{2,0,1:T(8,128)S(1)}, s32[]{:S(2)}) async-start(f32[256,16,128]{2,0,1:T(8,128)} %copy-done.4), calls=%async_computation.2 | async-start | bytes 2097152 | tf_op jit(solution)/shard_map/slice | solution.py:66
  100.2 3.2 slice-start
  108.8 11.7 %collective-permute-start.8 = (f32[32,2048]{1,0:T(8,128)}, f32[32,2048]{1,0:T(8,128)}, u32[]{:S(2)}, u32[]{:S(2)}) collective-permute-start(f32[32,2048]{1,0:T(8,128)} %bitcast.200), channel_id=1, source_target_pairs={{8,0},{16,8},{24,16},{32,24},{40,32},{48,40},{56,48},{64,56},{72,6... | collective-permute-start | bytes 786440 | tf_op jit(solution)/shard_map/ppermute | solution.py:13
  110.7 15.6 %collective-permute-start.10 = (f32[32,2048]{1,0:T(8,128)}, f32[32,2048]{1,0:T(8,128)}, u32[]{:S(2)}, u32[]{:S(2)}) collective-permute-start(f32[32,2048]{1,0:T(8,128)} %bitcast.198), channel_id=1, source_target_pairs={{24,0},{32,8},{40,16},{48,24},{56,32},{64,40},{72,48},{80,56},{88,... | collective-permute-start | bytes 786440 | tf_op jit(solution)/shard_map/ppermute | solution.py:13
  112.0 18.3 %collective-permute-start.11 = (f32[32,2048]{1,0:T(8,128)}, f32[32,2048]{1,0:T(8,128)}, u32[]{:S(2)}, u32[]{:S(2)}) collective-permute-start(f32[32,2048]{1,0:T(8,128)} %bitcast.197), channel_id=1, source_target_pairs={{32,0},{40,8},{48,16},{56,24},{64,32},{72,40},{80,48},{88,56},{96,... | collective-permute-start | bytes 786440 | tf_op jit(solution)/shard_map/ppermute | solution.py:13
  113.3 17.0 %collective-permute-start.9 = (f32[32,2048]{1,0:T(8,128)}, f32[32,2048]{1,0:T(8,128)}, u32[]{:S(2)}, u32[]{:S(2)}) collective-permute-start(f32[32,2048]{1,0:T(8,128)} %bitcast.235), channel_id=1, source_target_pairs={{16,0},{24,8},{32,16},{40,24},{48,32},{56,40},{64,48},{72,56},{80,... | collective-permute-start | bytes 786440 | tf_op jit(solution)/shard_map/ppermute | solution.py:13
  134.2 3.6 copy-start.1
  (11 other events, 23.5 us)
Sparse Core Ops, SparseCore 0:
  133.2 264.6 all-reduce.1
where the time goes:
time: 408 us; the launch traced here: 406 us
  waiting for transfers between devices  274 us (67%)
  local copies, waits for them, and re-layouts  44.6 us (11%)
  starting transfers between devices  43.8 us (11%)
  matrix products  24.5 us (6%)
  between operations  15.2 us (4%)
  other arithmetic  4.38 us (1%)
    psum x1, waiting for transfers between devices, local(): whole_sum = lax.psum(kernel_terms, ('seq', 'dp'))  256 us
    ppermute x16, starting transfers between devices, shifted(): lax.ppermute(value, axis, [(source, source + steps) for source in range(i...  43.8 us
    unnamed x52, local copies, waits for them, and re-layouts  18.1 us
    ppermute x16, waiting for transfers between devices, shifted(): lax.ppermute(value, axis, [(source, source + steps) for source in range(i...  17 us
  transfers between devices with their start and end apart: 17, of which 6 were waited for; matrix products, arithmetic and copies ran while one was open for 10% of the time, Pallas kernels for 0%

commit v1 on v0

v1 whole, which is shorter than its diff:
```python
import functools

import jax
import jax.numpy as jnp
from jax import lax
from jax.experimental import pallas as pl
from jax.experimental.pallas import tpu as pltpu
from jax.sharding import PartitionSpec as P

MESH = pl.DeviceIdType.MESH
H = 16
E = 128
SEG = 128
ROWS = SEG // 4
SLOTS = 4
HC = 4
NC = H // HC
WIDTH = H * E
BF = jnp.bfloat16
F32 = jnp.float32
SCALE = E ** -0.5
LOG2E = 1.4426950408889634
S1, S2, R1, R3, T1, T3, U1, U2 = range(8)


def nn(a, b):
    return lax.dot_general(a, b, (((1,), (0,)), ((), ())), preferred_element_type=F32)


def nt(a, b):
    return lax.dot_general(a, b, (((1,), (1,)), ((), ())), preferred_element_type=F32)


def tn(a, b):
    return lax.dot_general(a, b, (((0,), (0,)), ((), ())), preferred_element_type=F32)


def kernel(
    chips, books,
    q_hbm, k_hbm, v_hbm, g_hbm, w_hbm, reach,
    att_hbm, gq_hbm, gk_hbm, gv_hbm, gw_hbm,
    q_in, k_in, v_in, g_in, w_in,
    k_perm, v_perm, stacked, memory, bias, perms,
    slot_grads, sibling, totals, arrived, own,
    att_out, gq_out, gk_out, gv_out, gw_out,
    kg_half, kg_pair, kg_sent, kg_got, kg_books,
    load_sem, store_sem, send_sem, recv_sem, ring_send, ring_recv, book_send, book_recv,
):
    me = lax.axis_index("seq")
    book = lax.axis_index("dp")
    chip = me // 2
    core = me % 2
    twin = me + 1 - 2 * core

    def chip_at(step):
        return ((chip + step + chips) % chips) * 2 + core

    loads = [
        pltpu.make_async_copy(source, target, load_sem.at[i])
        for i, (source, target) in enumerate([
            (k_hbm.at[0], k_in), (v_hbm.at[0], v_in), (w_hbm, w_in), (q_hbm.at[0], q_in), (g_hbm.at[0], g_in),
        ])
    ]
    for load in loads:
        load.start()

    barrier = pltpu.get_barrier_semaphore()

    def greet(**where):
        pl.semaphore_signal(barrier, inc=1, device_id=where, device_id_type=MESH)

    greet(seq=twin)
    for step in range(1, chips):
        greet(seq=chip_at(step))
    for step in range(1, books):
        greet(dp=(book + step) % books)

    def push(kind, chunk, source, target, device):
        return pltpu.make_async_remote_copy(
            src_ref=source, dst_ref=target, send_sem=send_sem.at[kind, chunk], recv_sem=recv_sem.at[kind, chunk],
            device_id={"seq": device}, device_id_type=MESH,
        )

    def heads(chunk):
        return pl.ds(chunk * HC, HC)

    def cols(head, count=1):
        return pl.ds(head * E, count * E)

    links = {}
    for c in range(NC):
        links[S1, c] = push(S1, c, memory.at[0, heads(c)], memory.at[2, heads(c)], chip_at(1))
        links[S2, c] = push(S2, c, memory.at[0, heads(c)], memory.at[4, heads(c)], chip_at(2))
        links[R1, c] = push(R1, c, memory.at[2 * core, heads(c)], memory.at[1, heads(c)], twin)
        links[R3, c] = push(R3, c, memory.at[2 + 2 * core, heads(c)], memory.at[3, heads(c)], twin)
        links[T1, c] = push(T1, c, slot_grads.at[0, heads(c)], sibling.at[1 - core, heads(c)], twin)
        links[T3, c] = push(T3, c, slot_grads.at[2, heads(c)], sibling.at[2 - core, heads(c)], twin)
        links[U1, c] = push(U1, c, totals.at[0, heads(c)], arrived.at[0, heads(c)], chip_at(-1))
        links[U2, c] = push(U2, c, totals.at[1, heads(c)], arrived.at[1, heads(c)], chip_at(-2))

    sibling[2 - 2 * core] = jnp.zeros((H, 2 * ROWS, E), BF)

    row = lax.broadcasted_iota(jnp.int32, (SEG, SEG), 0)
    col = lax.broadcasted_iota(jnp.int32, (SEG, SEG), 1)
    row_key = 4 * (row % ROWS) + row // ROWS
    col_key = 4 * (col % ROWS) + col // ROWS
    perms[0] = jnp.where(col == row_key, 1.0, 0.0).astype(BF)
    perms[1] = jnp.where(row == col_key, 1.0, 0.0).astype(BF)
    slot = row // ROWS + 1
    seen = jnp.minimum(reach[0, 0], me)
    bias[0:SEG] = jnp.where(slot <= seen, 0.0, -1e30)
    bias[SEG:] = jnp.where(row_key <= col, 0.0, -1e30)

    def compress(c):
        span = cols(c * HC, HC)
        rows = []
        for source, target in ((k_in, k_perm), (v_in, v_perm)):
            moved = nn(perms[0], source[:, span]).astype(BF)
            for h in range(HC):
                one = moved[:, h * E:(h + 1) * E]
                target[c * HC + h] = one
                rows.append(jnp.concatenate([one[t * ROWS:(t + 1) * ROWS] for t in range(4)], axis=1))
        lhs = jnp.concatenate(rows, axis=0)
        stacked[c] = lhs
        packed = nn(lhs, w_in[...]).astype(BF)
        for h in range(HC):
            memory[0, c * HC + h, 0:ROWS] = packed[h * ROWS:(h + 1) * ROWS]
            memory[0, c * HC + h, ROWS:] = packed[(HC + h) * ROWS:(HC + h + 1) * ROWS]

    def attend(h):
        keys = jnp.concatenate([memory[r, h, 0:ROWS] for r in range(1, 5)] + [k_perm[h]], axis=0)
        values = jnp.concatenate([memory[r, h, ROWS:] for r in range(1, 5)] + [v_perm[h]], axis=0)
        query = q_in[:, cols(h)]
        grad = g_in[:, cols(h)]
        scores = nt(keys, query) * (SCALE * LOG2E) + bias[...]
        raised = jnp.exp2(scores - jnp.max(scores, axis=0, keepdims=True))
        weights = raised * (1.0 / jnp.sum(raised, axis=0, keepdims=True))
        low = weights.astype(BF)
        grad_weights = nt(values, grad)
        delta = jnp.sum(weights * grad_weights, axis=0, keepdims=True)
        grad_scores = (weights * (grad_weights - delta) * SCALE).astype(BF)
        att_out[:, cols(h)] = tn(low, values).astype(BF)
        gq_out[:, cols(h)] = tn(grad_scores, keys).astype(BF)
        for i, terms in enumerate((nn(grad_scores, query), nn(low, grad))):
            own[i, h] = terms[SEG:]
            for r in range(SLOTS):
                slot_grads[r, h, i * ROWS:(i + 1) * ROWS] = terms[r * ROWS:(r + 1) * ROWS].astype(BF)

    def combine(c):
        links[T1, c].wait_recv()
        links[T3, c].wait_recv()
        for i in range(2):
            totals[i, heads(c)] = (
                slot_grads[2 * i + 1, heads(c)].astype(F32) + sibling[i + 1, heads(c)].astype(F32)
            ).astype(BF)
        links[U1, c].start()
        links[U2, c].start()

    def finish(c, kernel_terms):
        links[U1, c].wait_recv()
        links[U2, c].wait_recv()
        memory_grads = (
            arrived[0, heads(c)].astype(F32) + arrived[1, heads(c)].astype(F32) + sibling[0, heads(c)].astype(F32)
        ).astype(BF)
        rows = jnp.concatenate(
            [memory_grads[h, i * ROWS:(i + 1) * ROWS] for i in range(2) for h in range(HC)], axis=0
        )
        terms = tn(stacked[c], rows)
        back = nt(rows, w_in[...])
        for i, out in enumerate((gk_out, gv_out)):
            pieces = []
            for h in range(HC):
                first = (i * HC + h) * ROWS
                spread = jnp.concatenate(
                    [back[first:first + ROWS, t * E:(t + 1) * E] for t in range(4)], axis=0
                )
                pieces.append((own[i, c * HC + h] + spread).astype(BF))
            out[:, cols(c * HC, HC)] = nn(perms[1], jnp.concatenate(pieces, axis=1)).astype(BF)
        return terms if kernel_terms is None else kernel_terms + terms

    for load in loads[:3]:
        load.wait()
    for c in range(NC):
        compress(c)
        if c == 0:
            pl.semaphore_wait(barrier, chips + books - 1)
        links[S1, c].start()
        links[S2, c].start()
    for load in loads[3:]:
        load.wait()

    kernel_terms = None
    for c in range(NC):
        links[S1, c].wait_recv()
        links[S2, c].wait_recv()
        links[R1, c].start()
        links[R3, c].start()
        links[R1, c].wait_recv()
        links[R3, c].wait_recv()
        for h in range(HC):
            attend(c * HC + h)
        links[T1, c].start()
        links[T3, c].start()
        if c >= 1:
            combine(c - 1)
        if c >= 2:
            kernel_terms = finish(c - 2, kernel_terms)
    stores = [
        pltpu.make_async_copy(source, target, store_sem.at[i])
        for i, (source, target) in enumerate([
            (att_out, att_hbm.at[0]), (gq_out, gq_hbm.at[0]), (gk_out, gk_hbm.at[0]), (gv_out, gv_hbm.at[0]),
            (gw_out, gw_hbm),
        ])
    ]
    stores[0].start()
    stores[1].start()
    combine(NC - 1)
    for c in range(max(NC - 2, 0), NC):
        kernel_terms = finish(c, kernel_terms)

    share = 4 * E // (2 * chips)
    for i in range(2 * chips):
        kg_half[i % 2, i // 2] = kernel_terms[i * share:(i + 1) * share]
    swap = pltpu.make_async_remote_copy(
        src_ref=kg_half.at[1 - core], dst_ref=kg_pair, send_sem=ring_send.at[0], recv_sem=ring_recv.at[0],
        device_id={"seq": twin}, device_id_type=MESH,
    )
    swap.start()
    stores[2].start()
    stores[3].start()
    swap.wait_recv()
    kg_sent[...] = (kg_half[core] + kg_pair[...]).astype(BF)
    around = []
    for step in range(1, chips):
        around.append(pltpu.make_async_remote_copy(
            src_ref=kg_sent.at[(chip + step) % chips], dst_ref=kg_got.at[step],
            send_sem=ring_send.at[step], recv_sem=ring_recv.at[step],
            device_id={"seq": chip_at(step)}, device_id_type=MESH,
        ))
    for copy in around:
        copy.start()
    total = kg_sent[chip].astype(F32)
    for step, copy in enumerate(around):
        copy.wait_recv()
        total = total + kg_got[step + 1].astype(F32)
    kg_books[book] = total
    across = []
    for step in range(1, books):
        across.append(pltpu.make_async_remote_copy(
            src_ref=kg_books.at[book], dst_ref=kg_books.at[book],
            send_sem=book_send.at[step], recv_sem=book_recv.at[step],
            device_id={"dp": (book + step) % books}, device_id_type=MESH,
        ))
    for copy in across:
        copy.start()
    for copy in across:
        copy.wait_recv()
    whole = kg_books[0]
    for i in range(1, books):
        whole = whole + kg_books[i]
    gw_out[...] = whole
    stores[4].start()
    for c in range(NC):
        for kind in range(8):
            links[kind, c].wait_send()
    swap.wait_send()
    for copy in around + across:
        copy.wait_send()
    for store in stores:
        store.wait()


def solution(mesh):
    chips = mesh.shape["seq"] // 2
    books = mesh.shape["dp"]

    def local(queries, key_vectors, value_vectors, cotangent, compress_kernel, memory_reach):
        share = 4 * E // (2 * chips)
        rows = jax.ShapeDtypeStruct((1, SEG, WIDTH), BF)
        anywhere = pl.BlockSpec(memory_space=pl.ANY)
        vm = pltpu.VMEM
        return pl.pallas_call(
            functools.partial(kernel, chips, books),
            out_shape=(rows, rows, rows, rows, jax.ShapeDtypeStruct((share, E), F32)),
            in_specs=[anywhere] * 5 + [pl.BlockSpec(memory_space=pltpu.SMEM)],
            out_specs=[anywhere] * 5,
            scratch_shapes=[
                *[vm((SEG, WIDTH), BF)] * 4, vm((4 * E, E), BF),
                vm((H, SEG, E), BF), vm((H, SEG, E), BF), vm((NC, 2 * HC * ROWS, 4 * E), BF),
                vm((5, H, 2 * ROWS, E), BF), vm((2 * SEG, SEG), F32), vm((2, SEG, SEG), BF),
                vm((SLOTS, H, 2 * ROWS, E), BF), vm((3, H, 2 * ROWS, E), BF), vm((2, H, 2 * ROWS, E), BF),
                vm((2, H, 2 * ROWS, E), BF), vm((2, H, SEG, E), F32),
                *[vm((SEG, WIDTH), BF)] * 4, vm((share, E), F32),
                vm((2, chips, share, E), F32), vm((chips, share, E), F32), vm((chips, share, E), BF),
                vm((chips, share, E), BF), vm((books, share, E), F32),
                pltpu.SemaphoreType.DMA((5,)), pltpu.SemaphoreType.DMA((5,)),
                pltpu.SemaphoreType.DMA((8, NC)), pltpu.SemaphoreType.DMA((8, NC)),
                pltpu.SemaphoreType.DMA((chips,)), pltpu.SemaphoreType.DMA((chips,)),
                pltpu.SemaphoreType.DMA((books,)), pltpu.SemaphoreType.DMA((books,)),
            ],
            compiler_params=pltpu.CompilerParams(collective_id=0, has_side_effects=True),
        )(queries, key_vectors, value_vectors, cotangent, compress_kernel, memory_reach)

    rows = P("dp", "seq", None)
    return jax.shard_map(
        local, mesh=mesh, in_specs=(rows, rows, rows, rows, P(), P("dp", "seq")),
        out_specs=(rows, rows, rows, rows, P("seq", None)), check_vma=False,
    )
```

time: 408 us -> 55.7 us (0.14)
  waiting for transfers between devices: 274 us -> 0 us
  Pallas kernels: 0 us -> 48.3 us
  starting transfers between devices: 43.8 us -> 0 us
  local copies, waits for them, and re-layouts: 44.6 us -> 5.8 us
  matrix products: 24.5 us -> 0 us
  between operations: 15.2 us -> 1.3 us
  other arithmetic: 4.38 us -> 0 us
    psum x1 -> x0, waiting for transfers between devices: 256 us -> none  [local(): whole_sum = lax.psum(kernel_terms, ('seq', 'dp'))]
    pallas_call x0 -> x1, Pallas kernels: none -> 48.3 us  [local(): pl.pallas_call(functools.partial(kernel, chips, books), out_shape=(rows,...]
    ppermute x16 -> x0, starting transfers between devices: 43.8 us -> none  [shifted(): lax.ppermute(value, axis, [(source, source + steps) for source in range(i...]
    dot_general x11 -> x0, matrix products: 21 us -> none  [the longest x1 6.47 us: attend_block(): jnp.einsum('hsl,shd->lhd', grad_scores, query_heads, preferred_element_ty...]
    ppermute x16 -> x0, waiting for transfers between devices: 17 us -> none  [shifted(): lax.ppermute(value, axis, [(source, source + steps) for source in range(i...]
    unnamed x52 -> x13, local copies, waits for them, and re-layouts: 18.1 us -> 5.8 us
    squeeze x8 -> x0, local copies, waits for them, and re-layouts: 7.66 us -> none  [the longest x4 4.77 us: local(): slot_keys[offset - 1]]
    reshape x4 -> x0, local copies, waits for them, and re-layouts: 7.52 us -> none  [the longest x2 3.83 us: local(): back_keys = jnp.einsum('mhf,tef->mthe', packed_grad_keys, kernel, preferr...]
  transfers between devices with their start and end apart: 17 -> 0, of which waited for: 6 -> 0; matrix products, arithmetic and copies ran while one was open for 10% -> 0% of each run, Pallas kernels for 0% -> 0%
where the time goes in v1:
time: 55.7 us; the launch traced here: 55.4 us
  Pallas kernels  48.3 us (87%)
  local copies, waits for them, and re-layouts  5.8 us (10%)
  between operations  1.3 us (2%)
    pallas_call x1, Pallas kernels, local(): pl.pallas_call(functools.partial(kernel, chips, books), out_shape=(rows,...  48.3 us
    unnamed x13, local copies, waits for them, and re-layouts  5.8 us

profile of v1, /device:TPU:1, one launch (start us, length us, event | category | flops | bytes accessed | tf_op | source)
XLA Modules:
  0.0 55.4 jit_solution(8971969907517109343)
XLA Ops:
  1.3 48.3 %shard_map.101 = (bf16[1,128,2048]{2,1,0:T(8,128)(2,1)}, bf16[1,128,2048]{2,1,0:T(8,128)(2,1)}, bf16[1,128,2048]{2,1,0:T(8,128)(2,1)}, bf16[1,128,2048]{2,1,0:T(8,128)(2,1)}, f32[16,128]{1,0:T(8,128)}) custom-call(bf16[1,128,2048]{2,1,0:T(8,128)(2,1)} %q_hbm.1, bf16[1,128,2048]{2,1,0:T(8,128)(2,1)} %k_hbm.1, bf16[1,128,2048]{2,1,0:T(8,128)(2,1)} %v_hbm.1, ...), custom_call_target="tpu_custom_call" | custom-call | tf_op jit(solution)/shard_map/pallas_call | solution.py:282
  49.6 0.0 copy-start.2
  49.6 1.9 %copy.17 = bf16[1,128,2048]{2,1,0:T(8,128)(2,1)} copy(bf16[1,128,2048]{2,1,0:T(8,128)(2,1)} %get-tuple-element.10) | data formatting | bytes 1048576
  51.6 0.0 copy-done.2
  51.6 0.0 copy-start.1
  51.6 0.8 %copy.18 = bf16[1,128,2048]{2,1,0:T(8,128)(2,1)} copy(bf16[1,128,2048]{2,1,0:T(8,128)(2,1)S(1)} %copy-done.2) | data formatting | bytes 1048576
  52.4 0.4 copy-done.1
  52.8 0.0 copy-start
  52.8 0.8 %copy.19 = bf16[1,128,2048]{2,1,0:T(8,128)(2,1)} copy(bf16[1,128,2048]{2,1,0:T(8,128)(2,1)S(1)} %copy-done.1) | data formatting | bytes 1048576
  53.6 0.4 copy-done
  54.0 0.0 copy-start.3
  54.0 0.8 %copy.20 = bf16[1,128,2048]{2,1,0:T(8,128)(2,1)} copy(bf16[1,128,2048]{2,1,0:T(8,128)(2,1)S(1)} %copy-done) | data formatting | bytes 1048576
  54.8 0.0 copy-done.3
  54.8 0.6 %copy.21 = f32[16,128]{1,0:T(8,128)} copy(f32[16,128]{1,0:T(8,128)S(1)} %copy-done.3) | data formatting | bytes 16384
Async XLA Ops:
  49.6 2.0 %copy-start.2 = (bf16[1,128,2048]{2,1,0:T(8,128)(2,1)S(1)}, bf16[1,128,2048]{2,1,0:T(8,128)(2,1)}, u32[]{:S(2)}) copy-start(bf16[1,128,2048]{2,1,0:T(8,128)(2,1)} %get-tuple-element.11) | copy-start | bytes 1572868
  51.6 1.2 %copy-start.1 = (bf16[1,128,2048]{2,1,0:T(8,128)(2,1)S(1)}, bf16[1,128,2048]{2,1,0:T(8,128)(2,1)}, u32[]{:S(2)}) copy-start(bf16[1,128,2048]{2,1,0:T(8,128)(2,1)} %get-tuple-element.12) | copy-start | bytes 1572868
  52.8 1.2 %copy-start = (bf16[1,128,2048]{2,1,0:T(8,128)(2,1)S(1)}, bf16[1,128,2048]{2,1,0:T(8,128)(2,1)}, u32[]{:S(2)}) copy-start(bf16[1,128,2048]{2,1,0:T(8,128)(2,1)} %get-tuple-element.13) | copy-start | bytes 1572868
  54.0 0.8 %copy-start.3 = (f32[16,128]{1,0:T(8,128)S(1)}, f32[16,128]{1,0:T(8,128)}, u32[]{:S(2)}) copy-start(f32[16,128]{1,0:T(8,128)} %get-tuple-element.14) | copy-start | bytes 24580

commit v2 on v1

--- a/solution.py
+++ b/solution.py
@@ -38,13 +38,12 @@
 def kernel(
     chips, books,
     q_hbm, k_hbm, v_hbm, g_hbm, w_hbm, reach,
-    att_hbm, gq_hbm, gk_hbm, gv_hbm, gw_hbm,
+    att_out, gq_out, gk_out, gv_out, gw_out,
     q_in, k_in, v_in, g_in, w_in,
     k_perm, v_perm, stacked, memory, bias, perms,
     slot_grads, sibling, totals, arrived, own,
-    att_out, gq_out, gk_out, gv_out, gw_out,
     kg_half, kg_pair, kg_sent, kg_got, kg_books,
-    load_sem, store_sem, send_sem, recv_sem, ring_send, ring_recv, book_send, book_recv,
+    load_sem, send_sem, recv_sem, ring_send, ring_recv, book_send, book_recv,
 ):
     me = lax.axis_index("seq")
     book = lax.axis_index("dp")
@@ -190,11 +189,16 @@
         load.wait()
 
     kernel_terms = None
-    for c in range(NC):
+    def relay(c):
         links[S1, c].wait_recv()
         links[S2, c].wait_recv()
         links[R1, c].start()
         links[R3, c].start()
+
+    relay(0)
+    for c in range(NC):
+        if c + 1 < NC:
+            relay(c + 1)
         links[R1, c].wait_recv()
         links[R3, c].wait_recv()
         for h in range(HC):
@@ -205,15 +209,6 @@
             combine(c - 1)
         if c >= 2:
             kernel_terms = finish(c - 2, kernel_terms)
-    stores = [
-        pltpu.make_async_copy(source, target, store_sem.at[i])
-        for i, (source, target) in enumerate([
-            (att_out, att_hbm.at[0]), (gq_out, gq_hbm.at[0]), (gk_out, gk_hbm.at[0]), (gv_out, gv_hbm.at[0]),
-            (gw_out, gw_hbm),
-        ])
-    ]
-    stores[0].start()
-    stores[1].start()
     combine(NC - 1)
     for c in range(max(NC - 2, 0), NC):
         kernel_terms = finish(c, kernel_terms)
@@ -226,8 +221,6 @@
         device_id={"seq": twin}, device_id_type=MESH,
     )
     swap.start()
-    stores[2].start()
-    stores[3].start()
     swap.wait_recv()
     kg_sent[...] = (kg_half[core] + kg_pair[...]).astype(BF)
     around = []
@@ -259,15 +252,21 @@
     for i in range(1, books):
         whole = whole + kg_books[i]
     gw_out[...] = whole
-    stores[4].start()
     for c in range(NC):
         for kind in range(8):
             links[kind, c].wait_send()
     swap.wait_send()
     for copy in around + across:
         copy.wait_send()
-    for store in stores:
-        store.wait()
+
+
+def store_kernel(*refs):
+    count = (len(refs) - 1) // 2
+    copies = [pltpu.make_async_copy(refs[i], refs[count + i], refs[-1].at[i]) for i in range(count)]
+    for copy in copies:
+        copy.start()
+    for copy in copies:
+        copy.wait()
 
 
 def solution(mesh):
@@ -276,30 +275,39 @@
 
     def local(queries, key_vectors, value_vectors, cotangent, compress_kernel, memory_reach):
         share = 4 * E // (2 * chips)
-        rows = jax.ShapeDtypeStruct((1, SEG, WIDTH), BF)
+        shapes = [((SEG, WIDTH), BF)] * 4 + [((share, E), F32)]
         anywhere = pl.BlockSpec(memory_space=pl.ANY)
+        local_memory = pl.BlockSpec(memory_space=pltpu.VMEM)
         vm = pltpu.VMEM
-        return pl.pallas_call(
+        results = pl.pallas_call(
             functools.partial(kernel, chips, books),
-            out_shape=(rows, rows, rows, rows, jax.ShapeDtypeStruct((share, E), F32)),
+            out_shape=tuple(vm(shape, kind) for shape, kind in shapes),
             in_specs=[anywhere] * 5 + [pl.BlockSpec(memory_space=pltpu.SMEM)],
-            out_specs=[anywhere] * 5,
+            out_specs=[local_memory] * 5,
             scratch_shapes=[
                 *[vm((SEG, WIDTH), BF)] * 4, vm((4 * E, E), BF),
                 vm((H, SEG, E), BF), vm((H, SEG, E), BF), vm((NC, 2 * HC * ROWS, 4 * E), BF),
                 vm((5, H, 2 * ROWS, E), BF), vm((2 * SEG, SEG), F32), vm((2, SEG, SEG), BF),
                 vm((SLOTS, H, 2 * ROWS, E), BF), vm((3, H, 2 * ROWS, E), BF), vm((2, H, 2 * ROWS, E), BF),
                 vm((2, H, 2 * ROWS, E), BF), vm((2, H, SEG, E), F32),
-                *[vm((SEG, WIDTH), BF)] * 4, vm((share, E), F32),
                 vm((2, chips, share, E), F32), vm((chips, share, E), F32), vm((chips, share, E), BF),
                 vm((chips, share, E), BF), vm((books, share, E), F32),
-                pltpu.SemaphoreType.DMA((5,)), pltpu.SemaphoreType.DMA((5,)),
+                pltpu.SemaphoreType.DMA((5,)),
                 pltpu.SemaphoreType.DMA((8, NC)), pltpu.SemaphoreType.DMA((8, NC)),
                 pltpu.SemaphoreType.DMA((chips,)), pltpu.SemaphoreType.DMA((chips,)),
                 pltpu.SemaphoreType.DMA((books,)), pltpu.SemaphoreType.DMA((books,)),
             ],
             compiler_params=pltpu.CompilerParams(collective_id=0, has_side_effects=True),
         )(queries, key_vectors, value_vectors, cotangent, compress_kernel, memory_reach)
+        results = [pltpu.with_memory_space_constraint(result, pltpu.VMEM) for result in results]
+        stored = pl.pallas_call(
+            store_kernel,
+            out_shape=tuple(jax.ShapeDtypeStruct(shape, kind) for shape, kind in shapes),
+            in_specs=[local_memory] * 5,
+            out_specs=[anywhere] * 5,
+            scratch_shapes=[pltpu.SemaphoreType.DMA((5,))],
+        )(*results)
+        return tuple(whole[None] for whole in stored[:4]) + (stored[4],)
 
     rows = P("dp", "seq", None)
     return jax.shard_map(

time: 55.7 us -> 50.4 us (0.905)
  local copies, waits for them, and re-layouts: 5.8 us -> 0 us
  Pallas kernels: 48.3 us -> 49 us
    unnamed x13 -> x0, local copies, waits for them, and re-layouts: 5.8 us -> none
    pallas_call x1 -> x2, Pallas kernels: 48.3 us -> 49 us  [the longest x1 47.6 us: local(): pl.pallas_call(functools.partial(kernel, chips, books), out_shape=tuple((...]
where the time goes in v2:
time: 50.4 us; the launch traced here: 50.3 us
  Pallas kernels  49 us (97%)
  between operations  1.29 us (3%)
    pallas_call x1, Pallas kernels, local(): pl.pallas_call(functools.partial(kernel, chips, books), out_shape=tuple((...  47.6 us
    pallas_call x1, Pallas kernels, local(): pl.pallas_call(store_kernel, out_shape=tuple((jax.ShapeDtypeStruct(shape,...  1.36 us

profile of v2, /device:TPU:1, one launch (start us, length us, event | category | flops | bytes accessed | tf_op | source)
XLA Modules:
  0.0 50.3 jit_solution(4682801901852620732)
XLA Ops:
  1.3 47.6 %shard_map.101 = (bf16[128,2048]{1,0:T(8,128)(2,1)S(1)}, bf16[128,2048]{1,0:T(8,128)(2,1)S(1)}, bf16[128,2048]{1,0:T(8,128)(2,1)S(1)}, bf16[128,2048]{1,0:T(8,128)(2,1)S(1)}, f32[16,128]{1,0:T(8,128)S(1)}) custom-call(bf16[1,128,2048]{2,1,0:T(8,128)(2,1)} %q_hbm.1, bf16[1,128,2048]{2,1,0:T(8,128)(2,1)} %k_hbm.1, bf16[1,128,2048]{2,1,0:T(8,128)(2,1)} %v_hbm.1, ...), custom_call_target="tpu_custom_call" | custom-call | tf_op jit(solution)/shard_map/pallas_call | solution.py:282
  48.9 1.4 %shard_map.102 = (bf16[128,2048]{1,0:T(8,128)(2,1)}, bf16[128,2048]{1,0:T(8,128)(2,1)}, bf16[128,2048]{1,0:T(8,128)(2,1)}, bf16[128,2048]{1,0:T(8,128)(2,1)}, f32[16,128]{1,0:T(8,128)}) custom-call(bf16[128,2048]{1,0:T(8,128)(2,1)S(1)} %get-tuple-element.15.refs_0_, bf16[128,2048]{1,0:T(8,128)(2,1)S(1)} %get-tuple-element.16.refs_1_, ...), custom_call_target="tpu_custom_call" | custom-call | tf_op jit(solution)/shard_map/pallas_call | solution.py:303

commit v3 on v2

v3 whole, which is shorter than its diff:
```python
import functools

import jax
import jax.numpy as jnp
from jax import lax
from jax.experimental import pallas as pl
from jax.experimental.pallas import tpu as pltpu
from jax.sharding import PartitionSpec as P

MESH = pl.DeviceIdType.MESH
H = 16
E = 128
SEG = 128
ROWS = SEG // 4
SLOTS = 4
HALF = H // 2
SIZES = (2, 2, 2, 2)
NC = len(SIZES)
FIRST = tuple(sum(SIZES[:c]) for c in range(NC))
FORWARD = (0, 1, 2, 3)
BACKWARD = (0, 1)
LAG = 1
WIDTH = H * E
SPAN = HALF * E
BF = jnp.bfloat16
F32 = jnp.float32
SCALE = E ** -0.5
LOG2E = 1.4426950408889634
S1, S2, F, U1, U2, KINDS = 0, 2, 4, 5, 6, 7
XP, XD, XQ, XG, XB, XO, SWAPS = 0, 1, 2, 3, 4, 5, 9


def nn(a, b):
    return lax.dot_general(a, b, (((1,), (0,)), ((), ())), preferred_element_type=F32)


def nt(a, b):
    return lax.dot_general(a, b, (((1,), (1,)), ((), ())), preferred_element_type=F32)


def tn(a, b):
    return lax.dot_general(a, b, (((0,), (0,)), ((), ())), preferred_element_type=F32)


def kernel(
    chips, books,
    q_hbm, k_hbm, v_hbm, g_hbm, w_hbm, reach,
    att_out, gq_out, gk_out, gv_out, gw_out,
    k_in, v_in, w_in, perms, perm, packed, memory, segments, sides, bias,
    totals, local, arrived, own, kept, summed, results,
    kg_half, kg_pair, kg_sent, kg_got, kg_books,
    load_sem, send_sem, recv_sem, swap_send, swap_recv, swap_local,
    ring_send, ring_recv, book_send, book_recv,
):
    me = lax.axis_index("seq")
    book = lax.axis_index("dp")
    chip = me // 2
    core = me % 2
    side = chip % 2
    twin = me + 1 - 2 * core

    def chip_at(step):
        return (chip + step + chips) % chips

    def seat(step):
        return chip_at(step) * 2 + core

    def half(which):
        return pl.ds(pl.multiple_of(which * SPAN, SPAN), SPAN)

    loads = [
        pltpu.make_async_copy(source, target, load_sem.at[i])
        for i, (source, target) in enumerate([(k_hbm.at[0], k_in), (v_hbm.at[0], v_in), (w_hbm, w_in)])
    ]
    for load in loads:
        load.start()

    barrier = pltpu.get_barrier_semaphore()

    def greet(**where):
        pl.semaphore_signal(barrier, inc=1, device_id=where, device_id_type=MESH)

    greet(seq=twin)
    for step in range(1, chips):
        greet(seq=seat(step))
    for step in range(1, 3):
        greet(seq=chip_at(step) * 2 + 1 - core)
        greet(seq=chip_at(-step) * 2 + 1 - core)
    for step in range(1, books):
        greet(dp=(book + step) % books)

    def heads(chunk, which=0):
        return pl.ds(which * HALF + FIRST[chunk], SIZES[chunk])

    def cols(head, count=1):
        return pl.ds(head * E, count * E)

    def push(source, target, sent, got, device):
        return pltpu.make_async_remote_copy(
            src_ref=source, dst_ref=target, send_sem=sent, recv_sem=got,
            device_id={"seq": device}, device_id_type=MESH,
        )

    def rows(c, first, count):
        return memory.at[heads(c), :, pl.ds(first, count)]

    own_row = pl.multiple_of(ROWS * core, ROWS)
    links = {}
    for c in range(NC):
        for j in range(2):
            links[S1 + j, c] = push(
                packed.at[heads(c, j)], rows(c, 2 * ROWS + own_row, ROWS),
                send_sem.at[S1 + j, c], recv_sem.at[S1 + core, c], chip_at(1) * 2 + j,
            )
            links[S2 + j, c] = push(
                packed.at[heads(c, j)], rows(c, own_row, ROWS),
                send_sem.at[S2 + j, c], recv_sem.at[S2 + core, c], chip_at(2) * 2 + j,
            )
        links[F, c] = push(
            rows(c, 0, 2 * ROWS), rows(c, 2 * ROWS, 2 * ROWS), send_sem.at[F, c], recv_sem.at[F, c], seat(-1),
        )
        links[U1, c] = push(
            totals.at[heads(c), :, pl.ds(2 * ROWS, 2 * ROWS)], arrived.at[0, heads(c)],
            send_sem.at[U1, c], recv_sem.at[U1, c], seat(1 - 2 * side) if c in BACKWARD else seat(-1),
        )
        links[U2, c] = push(
            totals.at[heads(c), :, pl.ds(0, 2 * ROWS)], arrived.at[1, heads(c)],
            send_sem.at[U2, c], recv_sem.at[U2, c], seat(-2),
        )

    def landed(kind, c):
        for k in range(2):
            push(
                packed.at[heads(c)], rows(c, 2 * ROWS if kind == S1 else 0, ROWS),
                send_sem.at[kind + k, c], recv_sem.at[kind + k, c], twin,
            ).wait_recv()

    def swap_pair(kind, mine, other, here, there):
        return (
            pltpu.make_async_copy(mine, here, swap_local.at[kind]),
            push(other, there, swap_send.at[kind], swap_recv.at[kind], twin),
        )

    def half_heads(which):
        return pl.ds(which * HALF, HALF)

    mid_rows = memory.at[:, :, pl.ds(4 * ROWS + own_row, ROWS)]
    swaps = {
        XP: swap_pair(XP, perm.at[half_heads(core)], perm.at[half_heads(1 - core)], segments.at[core], segments.at[core]),
        XD: swap_pair(XD, packed.at[half_heads(core)], packed.at[half_heads(1 - core)], mid_rows, mid_rows),
    }
    for kind, source in ((XQ, q_hbm), (XG, g_hbm)):
        target = sides.at[core, kind - XQ]
        swaps[kind] = swap_pair(kind, source.at[0, :, half(core)], source.at[0, :, half(1 - core)], target, target)
    for i, out in enumerate((att_out, gq_out, gk_out, gv_out)):
        target = out.at[:, half(core)]
        swaps[XO + i] = swap_pair(XO + i, results.at[i, core], results.at[i, 1 - core], target, target)
    open_rows = bias.at[core, pl.ds(0, SEG)]
    bias_swap = push(open_rows, open_rows, swap_send.at[XB], swap_recv.at[XB], twin)

    def hand_out(i):
        for copy in swaps[XO + i]:
            copy.start()

    swaps[XQ][0].start()
    swaps[XG][0].start()

    row = lax.broadcasted_iota(jnp.int32, (SEG, SEG), 0)
    col = lax.broadcasted_iota(jnp.int32, (SEG, SEG), 1)
    row_key = 4 * (row % ROWS) + row // ROWS
    col_key = 4 * (col % ROWS) + col // ROWS
    perms[0] = jnp.where(col == row_key, 1.0, 0.0).astype(BF)
    perms[1] = jnp.where(row == col_key, 1.0, 0.0).astype(BF)
    seen = jnp.minimum(reach[0, 0], me)
    bias[core, 0:SEG] = jnp.where(SLOTS - row // ROWS <= seen, 0.0, -1e30)
    causal = jnp.where(row_key <= col, 0.0, -1e30)
    bias[0, SEG:] = causal
    bias[1, SEG:] = causal

    def spread_lanes(one):
        return jnp.concatenate([one[t * ROWS:(t + 1) * ROWS] for t in range(4)], axis=1)

    def compress(c):
        size = SIZES[c]
        lhs, places = [], []
        for j in range(2):
            first = j * HALF + FIRST[c]
            for i, source in enumerate((k_in, v_in)):
                moved = nn(perms[0], source[:, cols(first, size)]).astype(BF)
                for h in range(size):
                    one = moved[:, h * E:(h + 1) * E]
                    perm[first + h, i] = one
                    lhs.append(spread_lanes(one))
                    places.append((first + h, i))
        out = nn(jnp.concatenate(lhs, axis=0), w_in[...]).astype(BF)
        for n, (h, i) in enumerate(places):
            packed[h, i] = out[n * ROWS:(n + 1) * ROWS]

    def listed(p, h, i):
        return jnp.concatenate([memory[h, i, p * ROWS:p * ROWS + SEG], segments[p, h, i]], axis=0)

    def score(h):
        pieces = []
        for p in range(2):
            query = sides[p, 0, :, cols(h)]
            grad = sides[p, 1, :, cols(h)]
            scores = nt(listed(p, h, 0), query) * (SCALE * LOG2E) + bias[p]
            raised = jnp.exp2(scores - jnp.max(scores, axis=0, keepdims=True))
            weights = raised * (1.0 / jnp.sum(raised, axis=0, keepdims=True))
            low = weights.astype(BF)
            grad_weights = nt(listed(p, h, 1), grad)
            delta = jnp.sum(weights * grad_weights, axis=0, keepdims=True)
            grad_scores = (weights * (grad_weights - delta) * SCALE).astype(BF)
            kept[p, 0, h] = grad_scores
            kept[p, 1, h] = low
            pieces.append((nn(grad_scores[:SEG], query), nn(low[:SEG], grad)))
        for i in range(2):
            left, right = pieces[0][i], pieces[1][i]
            totals[h, i, 0:ROWS] = left[:ROWS].astype(BF)
            totals[h, i, ROWS:] = (left[ROWS:] + right[:SEG - ROWS]).astype(BF)
            local[h, i] = right[SEG - ROWS:]

    def attend(h):
        for p in range(2):
            grad_scores, low = kept[p, 0, h], kept[p, 1, h]
            results[0, p, :, cols(h)] = tn(low, listed(p, h, 1)).astype(BF)
            results[1, p, :, cols(h)] = tn(grad_scores, listed(p, h, 0)).astype(BF)
            own[0, p, h] = nn(grad_scores[SEG:], sides[p, 0, :, cols(h)])
            own[1, p, h] = nn(low[SEG:], sides[p, 1, :, cols(h)])

    def combine(c):
        links[U1, c].start()
        if c in BACKWARD:
            pl.when(side == 0)(links[U2, c].start)
        else:
            links[U2, c].start()

    def carry(c):
        if c in BACKWARD:
            links[U1, c].wait_recv()

            @pl.when(side == 1)
            def _():
                totals[heads(c), :, 0:2 * ROWS] = (
                    totals[heads(c), :, 0:2 * ROWS].astype(F32) + arrived[0, heads(c)].astype(F32)
                ).astype(BF)
                links[U2, c].start()

    def chunk_heads(c):
        return range(FIRST[c], FIRST[c] + SIZES[c])

    def gather(c):
        if c not in BACKWARD:
            links[U1, c].wait_recv()
        links[U2, c].wait_recv()
        lhs, rhs = [], []
        for h in chunk_heads(c):
            near = arrived[0, h].astype(F32)
            if c in BACKWARD:
                near = jnp.where(side == 0, near, 0.0)
            whole = near + arrived[1, h].astype(F32)
            for i in range(2):
                one = jnp.concatenate([whole[i, :ROWS] + local[h, i], whole[i, ROWS:]], axis=0).astype(BF)
                summed[h, i] = one
                rhs.append(one)
                for p in range(2):
                    lhs.append(spread_lanes(segments[p, h, i]))
        return tn(jnp.concatenate(lhs, axis=0), jnp.concatenate(rhs, axis=0))

    def finish(c):
        size = SIZES[c]
        back = nt(jnp.concatenate([summed[h, i] for h in chunk_heads(c) for i in range(2)], axis=0), w_in[...])
        for i in range(2):
            for p in range(2):
                pieces = []
                for n, h in enumerate(chunk_heads(c)):
                    start = (4 * n + 2 * i + p) * ROWS
                    wide = jnp.concatenate(
                        [back[start:start + ROWS, t * E:(t + 1) * E] for t in range(4)], axis=0
                    )
                    pieces.append((own[i, p, h] + wide).astype(BF))
                results[2 + i, p, :, cols(FIRST[c], size)] = nn(
                    perms[1], jnp.concatenate(pieces, axis=1)
                ).astype(BF)

    def pass_on(c):
        if c in FORWARD:
            landed(S2, c)
            pl.when(side == 1)(links[F, c].start)

    def ready(c):
        if c in FORWARD:
            pl.when(side == 1)(lambda: landed(S1, c))
            pl.when(side == 0)(links[F, c].wait_recv)
        else:
            landed(S2, c)
            landed(S1, c)

    def send(c):
        for j in range(2):
            links[S2 + j, c].start()
        for j in range(2):
            if c in FORWARD:
                pl.when(side == 0)(links[S1 + j, c].start)
            else:
                links[S1 + j, c].start()

    for load in loads:
        load.wait()
    for c in range(NC):
        compress(c)
    pl.semaphore_wait(barrier, chips + books + 3)
    for c in range(NC):
        send(c)
    for kind in (XP, XD):
        for copy in swaps[kind]:
            copy.start()
    bias_swap.start()
    swaps[XQ][1].start()
    swaps[XG][1].start()
    for kind in (XP, XD, XQ, XG):
        swaps[kind][0].wait()
        swaps[kind][1].wait_recv()
    bias_swap.wait_recv()

    pass_on(0)
    pass_on(1)
    for c in range(NC):
        if c + 2 < NC:
            pass_on(c + 2)
        ready(c)
        for h in chunk_heads(c):
            score(h)
        combine(c)
        for h in chunk_heads(c):
            attend(h)
        if c >= LAG:
            carry(c - LAG)
    hand_out(0)
    hand_out(1)
    for c in range(NC - LAG, NC):
        carry(c)
    kernel_terms = gather(0)
    finish(0)
    for c in range(1, NC):
        kernel_terms = kernel_terms + gather(c)
        if c + 2 < NC:
            finish(c)

    share = 4 * E // (2 * chips)
    for i in range(2 * chips):
        kg_half[i % 2, i // 2] = kernel_terms[i * share:(i + 1) * share]
    swap = pltpu.make_async_remote_copy(
        src_ref=kg_half.at[1 - core], dst_ref=kg_pair, send_sem=ring_send.at[0], recv_sem=ring_recv.at[0],
        device_id={"seq": twin}, device_id_type=MESH,
    )
    swap.start()
    finish(NC - 2)
    swap.wait_recv()
    kg_sent[...] = (kg_half[core] + kg_pair[...]).astype(BF)
    around = []
    for step in range(1, chips):
        around.append(pltpu.make_async_remote_copy(
            src_ref=kg_sent.at[(chip + step) % chips], dst_ref=kg_got.at[step],
            send_sem=ring_send.at[step], recv_sem=ring_recv.at[step],
            device_id={"seq": seat(step)}, device_id_type=MESH,
        ))
    for copy in around:
        copy.start()
    finish(NC - 1)
    hand_out(2)
    hand_out(3)
    total = kg_sent[chip].astype(F32)
    for step, copy in enumerate(around):
        copy.wait_recv()
        total = total + kg_got[step + 1].astype(F32)
    kg_books[book] = total
    across = []
    for step in range(1, books):
        across.append(pltpu.make_async_remote_copy(
            src_ref=kg_books.at[book], dst_ref=kg_books.at[book],
            send_sem=book_send.at[step], recv_sem=book_recv.at[step],
            device_id={"dp": (book + step) % books}, device_id_type=MESH,
        ))
    for copy in across:
        copy.start()
    for copy in across:
        copy.wait_recv()
    whole = kg_books[0]
    for i in range(1, books):
        whole = whole + kg_books[i]
    gw_out[...] = whole
    for c in range(NC):
        for kind in (S2, S2 + 1, U1, U2):
            links[kind, c].wait_send()
        if c in FORWARD:
            pl.when(side == 1)(links[F, c].wait_send)
        for j in range(2):
            if c in FORWARD:
                pl.when(side == 0)(links[S1 + j, c].wait_send)
            else:
                links[S1 + j, c].wait_send()
    for kind in (XP, XD, XQ, XG):
        swaps[kind][1].wait_send()
    bias_swap.wait_send()
    for i in range(4):
        swaps[XO + i][0].wait()
        swaps[XO + i][1].wait()
    swap.wait_send()
    for copy in around + across:
        copy.wait_send()


def store_kernel(*refs):
    count = (len(refs) - 1) // 2
    copies = [pltpu.make_async_copy(refs[i], refs[count + i], refs[-1].at[i]) for i in range(count)]
    for copy in copies:
        copy.start()
    for copy in copies:
        copy.wait()


def solution(mesh):
    chips = mesh.shape["seq"] // 2
    books = mesh.shape["dp"]

    def local(queries, key_vectors, value_vectors, cotangent, compress_kernel, memory_reach):
        share = 4 * E // (2 * chips)
        shapes = [((SEG, WIDTH), BF)] * 4 + [((share, E), F32)]
        anywhere = pl.BlockSpec(memory_space=pl.ANY)
        local_memory = pl.BlockSpec(memory_space=pltpu.VMEM)
        vm = pltpu.VMEM
        results = pl.pallas_call(
            functools.partial(kernel, chips, books),
            out_shape=tuple(vm(shape, kind) for shape, kind in shapes),
            in_specs=[anywhere] * 5 + [pl.BlockSpec(memory_space=pltpu.SMEM)],
            out_specs=[local_memory] * 5,
            scratch_shapes=[
                vm((SEG, WIDTH), BF), vm((SEG, WIDTH), BF), vm((4 * E, E), BF), vm((2, SEG, SEG), BF),
                vm((H, 2, SEG, E), BF), vm((H, 2, ROWS, E), BF), vm((HALF, 2, 6 * ROWS, E), BF),
                vm((2, HALF, 2, SEG, E), BF), vm((2, 2, SEG, SPAN), BF), vm((2, 2 * SEG, SEG), F32),
                vm((HALF, 2, SEG, E), BF), vm((HALF, 2, ROWS, E), F32), vm((2, HALF, 2, 2 * ROWS, E), BF),
                vm((2, 2, HALF, SEG, E), F32), vm((2, 2, HALF, 2 * SEG, SEG), BF),
                vm((HALF, 2, 2 * ROWS, E), BF), vm((4, 2, SEG, SPAN), BF),
                vm((2, chips, share, E), F32), vm((chips, share, E), F32), vm((chips, share, E), BF),
                vm((chips, share, E), BF), vm((books, share, E), F32),
                pltpu.SemaphoreType.DMA((3,)),
                pltpu.SemaphoreType.DMA((KINDS, NC)), pltpu.SemaphoreType.DMA((KINDS, NC)),
                pltpu.SemaphoreType.DMA((SWAPS,)), pltpu.SemaphoreType.DMA((SWAPS,)), pltpu.SemaphoreType.DMA((SWAPS,)),
                pltpu.SemaphoreType.DMA((chips,)), pltpu.SemaphoreType.DMA((chips,)),
                pltpu.SemaphoreType.DMA((books,)), pltpu.SemaphoreType.DMA((books,)),
            ],
            compiler_params=pltpu.CompilerParams(collective_id=0, has_side_effects=True),
        )(queries, key_vectors, value_vectors, cotangent, compress_kernel, memory_reach)
        results = [pltpu.with_memory_space_constraint(result, pltpu.VMEM) for result in results]
        stored = pl.pallas_call(
            store_kernel,
            out_shape=tuple(jax.ShapeDtypeStruct(shape, kind) for shape, kind in shapes),
            in_specs=[local_memory] * 5,
            out_specs=[anywhere] * 5,
            scratch_shapes=[pltpu.SemaphoreType.DMA((5,))],
        )(*results)
        return tuple(whole[None] for whole in stored[:4]) + (stored[4],)

    rows = P("dp", "seq", None)
    return jax.shard_map(
        local, mesh=mesh, in_specs=(rows, rows, rows, rows, P(), P("dp", "seq")),
        out_specs=(rows, rows, rows, rows, P("seq", None)), check_vma=False,
    )
```

time: 50.4 us -> 45.7 us (0.907)
  Pallas kernels: 49 us -> 44.3 us
    pallas_call x1, Pallas kernels: 47.6 us -> 43 us  [local(): pl.pallas_call(functools.partial(kernel, chips, books), out_shape=tuple((...]
where the time goes in v3:
time: 45.7 us; the launch traced here: 45.6 us
  Pallas kernels  44.3 us (97%)
  between operations  1.29 us (3%)
    pallas_call x1, Pallas kernels, local(): pl.pallas_call(functools.partial(kernel, chips, books), out_shape=tuple((...  43 us
    pallas_call x1, Pallas kernels, local(): pl.pallas_call(store_kernel, out_shape=tuple((jax.ShapeDtypeStruct(shape,...  1.36 us

profile of v3, /device:TPU:1, one launch (start us, length us, event | category | flops | bytes accessed | tf_op | source)
XLA Modules:
  0.0 45.6 jit_solution(9931920988843209355)
XLA Ops:
  1.3 43.0 %shard_map.101 = (bf16[128,2048]{1,0:T(8,128)(2,1)S(1)}, bf16[128,2048]{1,0:T(8,128)(2,1)S(1)}, bf16[128,2048]{1,0:T(8,128)(2,1)S(1)}, bf16[128,2048]{1,0:T(8,128)(2,1)S(1)}, f32[16,128]{1,0:T(8,128)S(1)}) custom-call(bf16[1,128,2048]{2,1,0:T(8,128)(2,1)} %q_hbm.1, bf16[1,128,2048]{2,1,0:T(8,128)(2,1)} %k_hbm.1, bf16[1,128,2048]{2,1,0:T(8,128)(2,1)} %v_hbm.1, ...), custom_call_target="tpu_custom_call" | custom-call | tf_op jit(solution)/shard_map/pallas_call | solution.py:433
  44.2 1.4 %shard_map.102 = (bf16[128,2048]{1,0:T(8,128)(2,1)}, bf16[128,2048]{1,0:T(8,128)(2,1)}, bf16[128,2048]{1,0:T(8,128)(2,1)}, bf16[128,2048]{1,0:T(8,128)(2,1)}, f32[16,128]{1,0:T(8,128)}) custom-call(bf16[128,2048]{1,0:T(8,128)(2,1)S(1)} %get-tuple-element.15.refs_0_, bf16[128,2048]{1,0:T(8,128)(2,1)S(1)} %get-tuple-element.16.refs_1_, ...), custom_call_target="tpu_custom_call" | custom-call | tf_op jit(solution)/shard_map/pallas_call | solution.py:456

commit v4 on v3

--- a/solution.py
+++ b/solution.py
@@ -14,11 +14,11 @@
 ROWS = SEG // 4
 SLOTS = 4
 HALF = H // 2
-SIZES = (2, 2, 2, 2)
+SIZES = (1,) * HALF
 NC = len(SIZES)
 FIRST = tuple(sum(SIZES[:c]) for c in range(NC))
-FORWARD = (0, 1, 2, 3)
-BACKWARD = (0, 1)
+FORWARD = ()
+BACKWARD = ()
 LAG = 1
 WIDTH = H * E
 SPAN = HALF * E
@@ -72,22 +72,21 @@
         pltpu.make_async_copy(source, target, load_sem.at[i])
         for i, (source, target) in enumerate([(k_hbm.at[0], k_in), (v_hbm.at[0], v_in), (w_hbm, w_in)])
     ]
-    for load in loads:
-        load.start()
-
     barrier = pltpu.get_barrier_semaphore()
 
     def greet(**where):
         pl.semaphore_signal(barrier, inc=1, device_id=where, device_id_type=MESH)
 
-    greet(seq=twin)
-    for step in range(1, chips):
+    for step in range(books - 1, 0, -1):
+        greet(dp=(book + step) % books)
+    for step in sorted(range(1, chips), key=lambda one: -min(one, chips - one)):
         greet(seq=seat(step))
     for step in range(1, 3):
         greet(seq=chip_at(step) * 2 + 1 - core)
         greet(seq=chip_at(-step) * 2 + 1 - core)
-    for step in range(1, books):
-        greet(dp=(book + step) % books)
+    greet(seq=twin)
+    for load in loads:
+        load.start()
 
     def heads(chunk, which=0):
         return pl.ds(which * HALF + FIRST[chunk], SIZES[chunk])
@@ -309,22 +308,22 @@
         load.wait()
     for c in range(NC):
         compress(c)
-    pl.semaphore_wait(barrier, chips + books + 3)
-    for c in range(NC):
+        if c == 0:
+            pl.semaphore_wait(barrier, chips + books + 3)
         send(c)
-    for kind in (XP, XD):
-        for copy in swaps[kind]:
-            copy.start()
-    bias_swap.start()
-    swaps[XQ][1].start()
-    swaps[XG][1].start()
+        if c == 2:
+            for kind in (XQ, XG):
+                swaps[kind][1].start()
+            bias_swap.start()
+    for copy in swaps[XD] + swaps[XP]:
+        copy.start()
+
+    pass_on(0)
+    pass_on(1)
     for kind in (XP, XD, XQ, XG):
         swaps[kind][0].wait()
         swaps[kind][1].wait_recv()
     bias_swap.wait_recv()
-
-    pass_on(0)
-    pass_on(1)
     for c in range(NC):
         if c + 2 < NC:
             pass_on(c + 2)

time: 45.7 us -> 44.5 us (0.974)
  Pallas kernels: 44.3 us -> 43.1 us
    pallas_call x1, Pallas kernels: 43 us -> 41.8 us  [local(): pl.pallas_call(functools.partial(kernel, chips, books), out_shape=tuple((...]
where the time goes in v4:
time: 44.5 us; the launch traced here: 44.4 us
  Pallas kernels  43.1 us (97%)
  between operations  1.29 us (3%)
    pallas_call x1, Pallas kernels, local(): pl.pallas_call(functools.partial(kernel, chips, books), out_shape=tuple((...  41.8 us
    pallas_call x1, Pallas kernels, local(): pl.pallas_call(store_kernel, out_shape=tuple((jax.ShapeDtypeStruct(shape,...  1.36 us

profile of v4, /device:TPU:1, one launch (start us, length us, event | category | flops | bytes accessed | tf_op | source)
XLA Modules:
  0.0 44.4 jit_solution(4698402851753523035)
XLA Ops:
  1.3 41.8 %shard_map.101 = (bf16[128,2048]{1,0:T(8,128)(2,1)S(1)}, bf16[128,2048]{1,0:T(8,128)(2,1)S(1)}, bf16[128,2048]{1,0:T(8,128)(2,1)S(1)}, bf16[128,2048]{1,0:T(8,128)(2,1)S(1)}, f32[16,128]{1,0:T(8,128)S(1)}) custom-call(bf16[1,128,2048]{2,1,0:T(8,128)(2,1)} %q_hbm.1, bf16[1,128,2048]{2,1,0:T(8,128)(2,1)} %k_hbm.1, bf16[1,128,2048]{2,1,0:T(8,128)(2,1)} %v_hbm.1, ...), custom_call_target="tpu_custom_call" | custom-call | tf_op jit(solution)/shard_map/pallas_call | solution.py:432
  43.1 1.4 %shard_map.102 = (bf16[128,2048]{1,0:T(8,128)(2,1)}, bf16[128,2048]{1,0:T(8,128)(2,1)}, bf16[128,2048]{1,0:T(8,128)(2,1)}, bf16[128,2048]{1,0:T(8,128)(2,1)}, f32[16,128]{1,0:T(8,128)}) custom-call(bf16[128,2048]{1,0:T(8,128)(2,1)S(1)} %get-tuple-element.15.refs_0_, bf16[128,2048]{1,0:T(8,128)(2,1)S(1)} %get-tuple-element.16.refs_1_, ...), custom_call_target="tpu_custom_call" | custom-call | tf_op jit(solution)/shard_map/pallas_call | solution.py:455

commit v5 on v4

--- a/solution.py
+++ b/solution.py
@@ -297,12 +297,12 @@
 
     def send(c):
         for j in range(2):
-            links[S2 + j, c].start()
-        for j in range(2):
             if c in FORWARD:
                 pl.when(side == 0)(links[S1 + j, c].start)
             else:
                 links[S1 + j, c].start()
+        for j in range(2):
+            links[S2 + j, c].start()
 
     for load in loads:
         load.wait()
@@ -364,8 +364,8 @@
             send_sem=ring_send.at[step], recv_sem=ring_recv.at[step],
             device_id={"seq": seat(step)}, device_id_type=MESH,
         ))
-    for copy in around:
-        copy.start()
+    for step in sorted(range(1, chips), key=lambda one: -min(one, chips - one)):
+        around[step - 1].start()
     finish(NC - 1)
     hand_out(2)
     hand_out(3)
@@ -381,7 +381,7 @@
             send_sem=book_send.at[step], recv_sem=book_recv.at[step],
             device_id={"dp": (book + step) % books}, device_id_type=MESH,
         ))
-    for copy in across:
+    for copy in across[::-1]:
         copy.start()
     for copy in across:
         copy.wait_recv()

time: 44.5 us -> 44 us (0.989)
  Pallas kernels: 43.1 us -> 42.6 us
    pallas_call x1, Pallas kernels: 41.8 us -> 41.3 us  [local(): pl.pallas_call(functools.partial(kernel, chips, books), out_shape=tuple((...]
where the time goes in v5:
time: 44 us; the launch traced here: 43.9 us
  Pallas kernels  42.6 us (97%)
  between operations  1.29 us (3%)
    pallas_call x1, Pallas kernels, local(): pl.pallas_call(functools.partial(kernel, chips, books), out_shape=tuple((...  41.3 us
    pallas_call x1, Pallas kernels, local(): pl.pallas_call(store_kernel, out_shape=tuple((jax.ShapeDtypeStruct(shape,...  1.36 us

profile of v5, /device:TPU:1, one launch (start us, length us, event | category | flops | bytes accessed | tf_op | source)
XLA Modules:
  0.0 43.9 jit_solution(16476034580898722942)
XLA Ops:
  1.3 41.3 %shard_map.101 = (bf16[128,2048]{1,0:T(8,128)(2,1)S(1)}, bf16[128,2048]{1,0:T(8,128)(2,1)S(1)}, bf16[128,2048]{1,0:T(8,128)(2,1)S(1)}, bf16[128,2048]{1,0:T(8,128)(2,1)S(1)}, f32[16,128]{1,0:T(8,128)S(1)}) custom-call(bf16[1,128,2048]{2,1,0:T(8,128)(2,1)} %q_hbm.1, bf16[1,128,2048]{2,1,0:T(8,128)(2,1)} %k_hbm.1, bf16[1,128,2048]{2,1,0:T(8,128)(2,1)} %v_hbm.1, ...), custom_call_target="tpu_custom_call" | custom-call | tf_op jit(solution)/shard_map/pallas_call | solution.py:432
  42.6 1.4 %shard_map.102 = (bf16[128,2048]{1,0:T(8,128)(2,1)}, bf16[128,2048]{1,0:T(8,128)(2,1)}, bf16[128,2048]{1,0:T(8,128)(2,1)}, bf16[128,2048]{1,0:T(8,128)(2,1)}, f32[16,128]{1,0:T(8,128)}) custom-call(bf16[128,2048]{1,0:T(8,128)(2,1)S(1)} %get-tuple-element.15.refs_0_, bf16[128,2048]{1,0:T(8,128)(2,1)S(1)} %get-tuple-element.16.refs_1_, ...), custom_call_target="tpu_custom_call" | custom-call | tf_op jit(solution)/shard_map/pallas_call | solution.py:455

commit v6 on v5

--- a/solution.py
+++ b/solution.py
@@ -331,10 +331,13 @@
         for h in chunk_heads(c):
             score(h)
         combine(c)
-        for h in chunk_heads(c):
-            attend(h)
+        if c >= 1:
+            for h in chunk_heads(c - 1):
+                attend(h)
         if c >= LAG:
             carry(c - LAG)
+    for h in chunk_heads(NC - 1):
+        attend(h)
     hand_out(0)
     hand_out(1)
     for c in range(NC - LAG, NC):

time: 44 us -> 44 us (level)
  no operation moved by 1% of the time
where the time goes in v6:
time: 44 us; the launch traced here: 43.9 us
  Pallas kernels  42.6 us (97%)
  between operations  1.29 us (3%)
    pallas_call x1, Pallas kernels, local(): pl.pallas_call(functools.partial(kernel, chips, books), out_shape=tuple((...  41.3 us
    pallas_call x1, Pallas kernels, local(): pl.pallas_call(store_kernel, out_shape=tuple((jax.ShapeDtypeStruct(shape,...  1.36 us

profile of v6, /device:TPU:1, one launch (start us, length us, event | category | flops | bytes accessed | tf_op | source)
XLA Modules:
  0.0 43.9 jit_solution(17247642284412064957)
XLA Ops:
  1.3 41.3 %shard_map.101 = (bf16[128,2048]{1,0:T(8,128)(2,1)S(1)}, bf16[128,2048]{1,0:T(8,128)(2,1)S(1)}, bf16[128,2048]{1,0:T(8,128)(2,1)S(1)}, bf16[128,2048]{1,0:T(8,128)(2,1)S(1)}, f32[16,128]{1,0:T(8,128)S(1)}) custom-call(bf16[1,128,2048]{2,1,0:T(8,128)(2,1)} %q_hbm.1, bf16[1,128,2048]{2,1,0:T(8,128)(2,1)} %k_hbm.1, bf16[1,128,2048]{2,1,0:T(8,128)(2,1)} %v_hbm.1, ...), custom_call_target="tpu_custom_call" | custom-call | tf_op jit(solution)/shard_map/pallas_call | solution.py:435
  42.6 1.4 %shard_map.102 = (bf16[128,2048]{1,0:T(8,128)(2,1)}, bf16[128,2048]{1,0:T(8,128)(2,1)}, bf16[128,2048]{1,0:T(8,128)(2,1)}, bf16[128,2048]{1,0:T(8,128)(2,1)}, f32[16,128]{1,0:T(8,128)}) custom-call(bf16[128,2048]{1,0:T(8,128)(2,1)S(1)} %get-tuple-element.15.refs_0_, bf16[128,2048]{1,0:T(8,128)(2,1)S(1)} %get-tuple-element.16.refs_1_, ...), custom_call_target="tpu_custom_call" | custom-call | tf_op jit(solution)/shard_map/pallas_call | solution.py:458
